TPU v7x, 32 devices: a whole 2x2x4 slice. The times are simulated.
32 devices in a mesh: tm: 4 (over z), query: 2 (over y), rec: 4 (over x, core).
Axes of the slice: x: 2, y: 2, z: 4, core: 2. Of those that a mesh axis runs over, the one named last changes fastest.
Arguments:
- frames: bfloat16 [4, 2048, 1024], P('rec', 'tm'), may hold values from -100 to 100
- queries: bfloat16 [4096, 1024], P('query'), may hold values from -10 to 10
- kernel: float32 [33, 4096], P(None, 'query'), may hold values from 0.01 to 0.12
- labels: int32 [4, 2048], P('rec', 'tm'), may hold values from 0 to 4095
- lengths: int32 [4], P('rec'), may hold values from 512 to 2048, as said below
Outputs:
- grad_frames: bfloat16 [4, 2048, 1024], P('rec', 'tm', 'query')
- grad_queries: bfloat16 [4096, 1024], P('query', 'rec')
- grad_kernel: float32 [33, 4096], P(None, 'query')
Inputs may be any that keep to these rules, and one draw needn't show every extreme that they name: `lengths`: each entry counts the valid frames at the start of its recording; at least one recording has all 2048 frames valid.
All inputs are finite; a program needn't handle non-finite values.
Results may differ from a plain program's by a relative error of at most 0.0049.
Values sent between devices are 32-bit elements; how exact they have to be, the bound alone decides.
A program may use at most 64 MiB of HBM per device.

v0:
```python
import math
import jax
import jax.numpy as jnp
from jax import lax
from jax.sharding import PartitionSpec as P


def merged(x, axis, combine):
    everything = jax.tree.map(lambda part: lax.all_gather(part, axis), x)
    first = jax.tree.map(lambda part: part[0], everything)

    def step(k, so_far):
        return combine(so_far, jax.tree.map(lambda part: part[k], everything))

    return lax.fori_loop(1, lax.axis_size(axis), step, first)


def with_halo(x, sides, width):
    for axis, dim in sides:
        peers, length = (lax.axis_size(axis), x.shape[dim])
        up = [(i, (i + 1) % peers) for i in range(peers - 1)]
        down = [(j, i) for i, j in up]
        last = lax.slice_in_dim(x, length - width, length, axis=dim)
        first = lax.slice_in_dim(x, 0, width, axis=dim)
        before = lax.ppermute(last, axis, up)
        after = lax.ppermute(first, axis, down)
        x = jnp.concatenate([before, x, after], axis=dim)
    return x


def tap_sum(kernel, padded, row_count, flipped):
    tap_count = kernel.shape[0]
    running = jnp.zeros((row_count, padded.shape[1]), jnp.float32)
    for offset in range(tap_count):
        begin_row = tap_count - 1 - offset if flipped else offset
        running = running + kernel[offset][None, :] * padded[begin_row : begin_row + row_count]
    return running


def combine_stats(first_pair, second_pair):
    top_value = jnp.maximum(first_pair[0], second_pair[0])
    total_value = first_pair[1] * jnp.exp(first_pair[0] - top_value) + second_pair[1] * jnp.exp(
        second_pair[0] - top_value
    )
    return (top_value, total_value)


def row_softmax(smooth):
    local_top = jnp.max(smooth, axis=1)
    local_total = jnp.sum(jnp.exp(smooth - local_top[:, None]), axis=1)
    top_value, total_value = merged((local_top, local_total), "query", combine_stats)
    return jnp.exp(smooth - top_value[:, None]) / total_value[:, None]


def per_device(frames, queries, kernel, labels, lengths):
    frame_rows = frames[0]
    label_ids = labels[0]
    length_now = lengths[0]
    row_count = frame_rows.shape[0]
    query_count = queries.shape[0]
    width = frame_rows.shape[1]
    tap_count = kernel.shape[0]
    rim_width = tap_count // 2
    logit_scale = 10.0 / math.sqrt(width)
    frame_start = lax.axis_index("tm") * row_count
    is_valid = frame_start + jnp.arange(row_count, dtype=jnp.int32) < length_now
    query_start = lax.axis_index("query") * query_count
    query_ids = query_start + jnp.arange(query_count, dtype=jnp.int32)
    scores = (
        lax.dot_general(
            frame_rows, queries, (((1,), (1,)), ((), ())), preferred_element_type=jnp.float32
        )
        * logit_scale
    )
    scores = jnp.where(is_valid[:, None], scores, 0.0)
    wide = with_halo(scores, (("tm", 0),), 2 * rim_width)
    label_pad = with_halo(label_ids, (("tm", 0),), rim_width)
    ext_rows = row_count + 2 * rim_width
    ext_frames = frame_start - rim_width + jnp.arange(ext_rows, dtype=jnp.int32)
    ext_valid = (ext_frames >= 0) & (ext_frames < length_now)
    smooth = tap_sum(kernel, wide, ext_rows, False)
    softmax_out = row_softmax(smooth)
    positive = (label_pad[:, None] == query_ids[None, :]).astype(jnp.float32)
    grad_pad = jnp.where(ext_valid[:, None], softmax_out - positive, 0.0)
    map_grad = grad_pad[rim_width : rim_width + row_count]
    padded = wide[rim_width : rim_width + row_count + 2 * rim_width]
    score_grad = tap_sum(kernel, grad_pad, row_count, True)
    score_grad = jnp.where(is_valid[:, None], score_grad, 0.0).astype(jnp.bfloat16)
    frame_part = jnp.dot(score_grad, queries, preferred_element_type=jnp.float32)
    frame_sum = lax.psum_scatter(frame_part, "query", scatter_dimension=1, tiled=True)
    grad_frames = (frame_sum * logit_scale).astype(jnp.bfloat16)[None]
    query_part = lax.dot_general(
        score_grad, frame_rows, (((0,), (0,)), ((), ())), preferred_element_type=jnp.float32
    )
    kernel_part = jnp.stack(
        [
            jnp.sum(map_grad * padded[offset : offset + row_count], axis=0)
            for offset in range(tap_count)
        ]
    )
    query_whole, grad_kernel = lax.psum((query_part, kernel_part), ("tm", "rec"))
    col_count = width // lax.axis_size("rec")
    query_cols = lax.dynamic_slice_in_dim(
        query_whole, lax.axis_index("rec") * col_count, col_count, 1
    )
    grad_queries = (query_cols * logit_scale).astype(jnp.bfloat16)
    return (grad_frames, grad_queries, grad_kernel)


def solution(mesh):
    in_specs = (P("rec", "tm", None), P("query", None), P(None, "query"), P("rec", "tm"), P("rec"))
    out_specs = (P("rec", "tm", "query"), P("query", "rec"), P(None, "query"))
    return jax.shard_map(
        per_device, mesh=mesh, in_specs=in_specs, out_specs=out_specs, check_vma=False
    )
```

profile of v0, /device:TPU:0, one launch (start us, length us, event | category | flops | bytes accessed | tf_op | source)
XLA Modules:
  0.0 326.1 jit_solution(487026478341481205)
XLA Ops:
  8.0 0.0 copy-start
  8.0 0.0 reduce-scatter.2.cloned.1.call-start
  8.1 0.8 slice_bitcast_fusion.1
  8.9 4.9 %collective-permute-start.2 = (s32[16]{0:T(128)S(1)}, s32[16]{0:T(128)S(1)}, u32[]{:S(2)}, u32[]{:S(2)}) collective-permute-start(s32[16]{0:T(128)S(1)} %get-tuple-element.101), channel_id=1, source_target_pairs={{0,8},{8,16},{16,24},{1,9},{9,17},{17,25},{2,10},{10,18},{18,26},{... | collective-permute-start | bytes 200 | tf_op jit(solution)/shard_map/ppermute | solution.py:25
  13.8 1.3 collective-permute-start.3
  15.8 0.0 copy-done
  15.8 0.0 copy-start.7
  15.8 0.0 copy-start.10
  15.8 0.0 copy-start.8
  15.8 4.6 %multiply_select_fusion = f32[512,2048]{1,0:T(8,128)S(1)} fusion(bf16[2048,1024]{1,0:T(8,128)(2,1)} %param.6, pred[512]{0:T(512)(128)(4,1)S(1)} %add_compare_fusion, bf16[1,512,1024]{2,1,0:T(8,128)(2,1)S(1)} %copy-done), kind=kOutput, calls=%fused_computation.265 | convolution fusion | flops 2149580800 | bytes 9437696 | tf_op jit(solution)/shard_map/dot_general | solution.py:70
  20.5 0.0 copy-start.3
  20.5 2.0 copy-done.3
  22.5 4.6 %collective-permute-start = (f32[32,2048]{1,0:T(8,128)S(1)}, f32[32,2048]{1,0:T(8,128)S(1)}, u32[]{:S(2)}, u32[]{:S(2)}) collective-permute-start(f32[32,2048]{1,0:T(8,128)S(1)} %get-tuple-element.66), channel_id=1, source_target_pairs={{0,8},{8,16},{16,24},{1,9},{9,17},{17,25},{2,10},{10,18},{18,26},{... | collective-permute-start | bytes 786440 | tf_op jit(solution)/shard_map/ppermute | solution.py:25
  27.0 1.3 collective-permute-start.1
  28.3 0.0 copy-done.7
  28.3 0.1 fusion.176
  28.4 0.1 fusion.175
  28.6 0.0 copy-done.10
  28.6 0.6 dynamic-slice
  29.8 0.0 collective-permute-done.2
  29.8 0.0 collective-permute-done.3
  29.9 0.0 copy-done.8
  29.9 0.1 pad_add_fusion
  29.9 0.0 copy-start.4
  29.9 2.1 collective-permute-done
  32.0 4.1 %collective-permute-done.1 = f32[32,2048]{1,0:T(8,128)S(1)} collective-permute-done((f32[32,2048]{1,0:T(8,128)S(1)}, f32[32,2048]{1,0:T(8,128)S(1)}, u32[]{:S(2)}, u32[]{:S(2)}) %collective-permute-start.1) | collective-permute-done | bytes 262176 | tf_op jit(solution)/shard_map/ppermute | solution.py:26
  36.1 2.8 pad_maximum_fusion.2
  38.9 0.0 copy-done.4
  38.9 22.3 %fusion.172 = (f32[544]{0:T(1024)S(1)}, f32[544,2048]{1,0:T(8,128)S(1)}) fusion(f32[32,2048]{1,0:T(8,128)S(1)} %collective-permute-done.1, f32[512,2048]{1,0:T(8,128)S(1)} %copy-done.4, f32[2048]{0:T(1024)S(1)} %bitcast.110, f32[576,2048]{1,0:T(8,128)S(1)} %pad_maximum_fusion.2, f32[2048]{0:T(1024)S(1)} %bitcast.112, f32[2048]{0:T(1024)S(1)} %bitcast.116, ...), kind=kLoop, calls=%fused_computation.285 | loop fusion | flops 75759072 | bytes 147597440 | tf_op jit(solution)/shard_map/reduce_max | solution.py:49
  61.2 0.0 copy-start.6
  61.2 2.0 copy-done.6
  63.2 0.7 exponential_reduce_fusion
  64.0 0.3 dynamic-update-slice
  64.3 0.3 dynamic-update-slice.1
  64.6 8.1 %all-reduce.3 = (f32[1088]{0:T(1024)S(1)}, f32[1088]{0:T(1024)S(1)}) all-reduce(f32[1088]{0:T(1024)S(1)} %dynamic-update-slice.1, f32[1088]{0:T(1024)S(1)} %dynamic-update-slice), channel_id=3, replica_groups=mesh['tm'=4,'query'=2,'rec'=4] {'query'}, use_global_device_ids=true, to_apply=%add.1 | all-reduce | flops 2176 | bytes 17408
  72.6 0.1 fusion.168
  72.7 3.1 subtract_select_fusion
  75.8 0.0 copy-start.1
  75.8 0.0 copy-start.9
  75.9 18.4 %fusion.132 = bf16[512,2048]{1,0:T(8,128)(2,1)} fusion(f32[544,2048]{1,0:T(8,128)S(1)} %subtract_select_fusion, f32[2048]{0:T(1024)S(1)} %bitcast.111, f32[2048]{0:T(1024)S(1)} %bitcast.113, f32[2048]{0:T(1024)S(1)} %bitcast.117, f32[2048]{0:T(1024)S(1)} %bitcast.119, f32[2048]{0:T(1024)S(1)} %bitcast.121, f32[2048]{0:T(1024)S(1)} %bitcast.123, ...), kind=kLoop, calls=%fused_computation.201 | loop fusion | flops 70254592 | bytes 140780032 | tf_op jit(solution)/shard_map/convert_element_type | solution.py:88
  94.2 0.0 copy-done.1
  94.2 0.0 copy-done.9
  94.2 5.3 %fusion.177 = f32[512,1024]{1,0:T(8,128)} fusion(bf16[512,2048]{1,0:T(8,128)(2,1)} %fusion.132, bf16[2048,1024]{1,0:T(8,128)(2,1)S(1)} %copy-done.9), kind=kOutput, calls=%fused_computation.289 | convolution fusion | flops 2147483648 | bytes 8388608 | tf_op jit(solution)/shard_map/dot_general | solution.py:89
  99.5 0.0 reduce-scatter.2.cloned.1.call-update
  99.6 0.3 all-reduce.6.cloned.1.call-start
  99.8 0.0 copy-start.2
  99.8 0.0 copy-start.5
  99.9 12.5 %fusion.129 = (f32[2048]{0:T(1024)S(1)}, f32[2048]{0:T(1024)S(1)}, f32[2048]{0:T(1024)S(1)}, f32[2048]{0:T(1024)S(1)}, f32[2048]{0:T(1024)S(1)}, /*index=5*/f32[2048]{0:T(1024)S(1)}) fusion(f32[32,2048]{1,0:T(8,128)S(1)} %collective-permute-done, f32[512,2048]{1,0:T(8,128)} %copy-done.3, f32[544,2048]{1,0:T(8,128)} %copy-done.1), kind=kLoop, calls=%fused_computation.197 | loop fusion | flops 18862080 | bytes 8699904 | tf_op jit(solution)/shard_map/reduce_sum | solution.py:97
  112.3 0.0 copy-done.2
  112.3 0.2 copy-done.5
  112.6 3.8 %fusion.78 = (f32[2048]{0:T(1024)S(1)}, f32[2048]{0:T(1024)S(1)}, f32[2048]{0:T(1024)S(1)}, f32[2048]{0:T(1024)S(1)}, f32[2048]{0:T(1024)S(1)}, /*index=5*/f32[2048]{0:T(1024)S(1)}) fusion(f32[32,2048]{1,0:T(8,128)S(1)} %collective-permute-done.1, f32[512,2048]{1,0:T(8,128)S(1)} %copy-done.5, f32[544,2048]{1,0:T(8,128)S(1)} %copy-done.2), kind=kLoop, calls=%fused_computation.146 | loop fusion | flops 18862080 | bytes 8699904 | tf_op jit(solution)/shard_map/reduce_sum | solution.py:97
  116.4 3.8 %fusion.81 = (f32[2048]{0:T(1024)S(1)}, f32[2048]{0:T(1024)S(1)}, f32[2048]{0:T(1024)S(1)}, f32[2048]{0:T(1024)S(1)}, f32[2048]{0:T(1024)S(1)}, /*index=5*/f32[2048]{0:T(1024)S(1)}) fusion(f32[32,2048]{1,0:T(8,128)S(1)} %collective-permute-done.1, f32[512,2048]{1,0:T(8,128)S(1)} %copy-done.5, f32[544,2048]{1,0:T(8,128)S(1)} %copy-done.2), kind=kLoop, calls=%fused_computation.149 | loop fusion | flops 18862080 | bytes 8699904 | tf_op jit(solution)/shard_map/reduce_sum | solution.py:97
  120.2 3.2 fusion.126
  123.4 5.4 %fusion.75 = (f32[2048]{0:T(1024)S(1)}, f32[2048]{0:T(1024)S(1)}, f32[2048]{0:T(1024)S(1)}, f32[2048]{0:T(1024)S(1)}, f32[2048]{0:T(1024)S(1)}, /*index=5*/f32[2...) fusion(f32[32,2048]{1,0:T(8,128)S(1)} %collective-permute-done.1, f32[512,2048]{1,0:T(8,128)S(1)} %copy-done.5, ...), kind=kLoop, calls=%fused_computation.143 | loop fusion | flops 27244544 | bytes 8986624 | tf_op jit(solution)/shard_map/reduce_sum | solution.py:97
  128.8 3.5 %stack.135 = f32[33,2048]{1,0:T(8,128)} concatenate(f32[1,2048]{1,0:T(1,128)S(1)} %bitcast.162, f32[1,2048]{1,0:T(1,128)S(1)} %bitcast.163, f32[1,2048]{1,0:T(1,128)S(1)} %bitcast.164, f32[1,2048]{1,0:T(1,128)S(1)} %bitcast.165, f32[1,2048]{1,0:T(1,128)S(1)} %bitcast.166, f32[1,2048]{1,0:T(1,128)S(1)} %bitcast.180, f32[1,2048]{1,0:T(1,128)S(1)} %bitcast.181, ...), dimensions={0} | concatenate | bytes 540672 | tf_op jit(solution)/shard_map/stack | solution.py:95
  132.4 7.2 %fusion.164 = f32[2048,1024]{1,0:T(8,128)} fusion(bf16[512,2048]{1,0:T(8,128)(2,1)} %fusion.132, bf16[1,512,1024]{2,1,0:T(8,128)(2,1)S(1)} %copy-done), kind=kOutput, calls=%fused_computation.267 | convolution fusion | flops 2147483648 | bytes 11534336 | tf_op jit(solution)/shard_map/dot_general | solution.py:92
  139.6 0.0 all-reduce.6.cloned.1.call-update
  139.6 0.0 reduce-scatter.2.cloned.1.call-done
  139.6 2.1 fusion.167
  141.8 172.5 %all-reduce.6.cloned.1.call-done = (f32[2048,1024]{1,0:T(8,128)}, f32[33,2048]{1,0:T(8,128)}) async-done(((f32[2048,1024]{1,0:T(8,128)}, f32[33,2048]{1,0:T(8,128)}), (f32[2048,1024]{1,0:T(8,128)}, f32[33,2048]{1,0:T(8,128)})) %all-reduce.6.cloned.1.call-update) | async-done | bytes 8658960 | tf_op jit(solution)/shard_map/psum | solution.py:101
  314.2 2.7 multiply_convert_fusion
  317.0 1.7 copy.13
  (6 shorter events, 0.1 us)
Async XLA Ops:
  8.0 7.8 %copy-start = (bf16[1,512,1024]{2,1,0:T(8,128)(2,1)S(1)}, bf16[1,512,1024]{2,1,0:T(8,128)(2,1)}, u32[]{:S(2)}) copy-start(bf16[1,512,1024]{2,1,0:T(8,128)(2,1)} %param.5) | copy-start | bytes 3145732
  8.0 131.6 %reduce-scatter.2.cloned.1.call-start = ((), (), s32[]{:S(2)}) async-start(), calls=%async_computation.1 | async-start | bytes 3145728 | tf_op jit(solution)/shard_map/reduce_scatter | solution.py:90
  8.9 21.0 %collective-permute-start.2 = (s32[16]{0:T(128)S(1)}, s32[16]{0:T(128)S(1)}, u32[]{:S(2)}, u32[]{:S(2)}) collective-permute-start(s32[16]{0:T(128)S(1)} %get-tuple-element.101), channel_id=1, source_target_pairs={{0,8},{8,16},{16,24},{1,9},{9,17},{17,25},{2,10},{10,18},{18,26},{... | collective-permute-start | bytes 200 | tf_op jit(solution)/shard_map/ppermute | solution.py:25
  13.8 16.0 %collective-permute-start.3 = (s32[16]{0:T(128)S(1)}, s32[16]{0:T(128)S(1)}, u32[]{:S(2)}, u32[]{:S(2)}) collective-permute-start(s32[16]{0:T(128)S(1)} %get-tuple-element.102), channel_id=1, source_target_pairs={{8,0},{16,8},{24,16},{9,1},{17,9},{25,17},{10,2},{18,10},{26,18},{... | collective-permute-start | bytes 200 | tf_op jit(solution)/shard_map/ppermute | solution.py:26
  15.8 12.5 %copy-start.7 = (f32[33,2048]{1,0:T(8,128)S(1)}, f32[33,2048]{1,0:T(8,128)}, u32[]{:S(2)}) copy-start(f32[33,2048]{1,0:T(8,128)} %param.7) | copy-start | bytes 811012
  15.8 12.8 %copy-start.10 = (u32[32]{0:T(128)S(1)}, u32[32]{0:T(128)}, u32[]{:S(2)}) copy-start(u32[32]{0:T(128)} %constant.48) | copy-start | bytes 388
  15.8 14.0 %copy-start.8 = (s32[1,512]{1,0:T(1,128)S(1)}, s32[1,512]{1,0:T(1,128)}, u32[]{:S(2)}) copy-start(s32[1,512]{1,0:T(1,128)} %param.8) | copy-start | bytes 6148
  20.5 2.0 copy-start.3
  22.5 9.5 %collective-permute-start = (f32[32,2048]{1,0:T(8,128)S(1)}, f32[32,2048]{1,0:T(8,128)S(1)}, u32[]{:S(2)}, u32[]{:S(2)}) collective-permute-start(f32[32,2048]{1,0:T(8,128)S(1)} %get-tuple-element.66), channel_id=1, source_target_pairs={{0,8},{8,16},{16,24},{1,9},{9,17},{17,25},{2,10},{10,18},{18,26},{... | collective-permute-start | bytes 786440 | tf_op jit(solution)/shard_map/ppermute | solution.py:25
  27.0 9.1 %collective-permute-start.1 = (f32[32,2048]{1,0:T(8,128)S(1)}, f32[32,2048]{1,0:T(8,128)S(1)}, u32[]{:S(2)}, u32[]{:S(2)}) collective-permute-start(f32[32,2048]{1,0:T(8,128)S(1)} %get-tuple-element.67), channel_id=1, source_target_pairs={{8,0},{16,8},{24,16},{9,1},{17,9},{25,17},{10,2},{18,10},{26,18},{... | collective-permute-start | bytes 786440 | tf_op jit(solution)/shard_map/ppermute | solution.py:26
  29.9 9.0 %copy-start.4 = (f32[512,2048]{1,0:T(8,128)S(1)}, f32[512,2048]{1,0:T(8,128)}, u32[]{:S(2)}) copy-start(f32[512,2048]{1,0:T(8,128)} %copy-done.3) | copy-start | bytes 12582916
  61.2 2.0 copy-start.6
  75.8 18.4 %copy-start.1 = (f32[544,2048]{1,0:T(8,128)}, f32[544,2048]{1,0:T(8,128)S(1)}, u32[]{:S(2)}) copy-start(f32[544,2048]{1,0:T(8,128)S(1)} %subtract_select_fusion) | copy-start | bytes 13369348
  75.8 18.4 %copy-start.9 = (bf16[2048,1024]{1,0:T(8,128)(2,1)S(1)}, bf16[2048,1024]{1,0:T(8,128)(2,1)}, u32[]{:S(2)}) copy-start(bf16[2048,1024]{1,0:T(8,128)(2,1)} %param.6) | copy-start | bytes 12582916
  99.6 214.7 %all-reduce.6.cloned.1.call-start = ((), (), s32[]{:S(2)}) async-start(), calls=%async_computation.2 | async-start | bytes 17432576 | tf_op jit(solution)/shard_map/psum | solution.py:101
  99.8 12.5 %copy-start.2 = (f32[544,2048]{1,0:T(8,128)S(1)}, f32[544,2048]{1,0:T(8,128)}, u32[]{:S(2)}) copy-start(f32[544,2048]{1,0:T(8,128)} %copy-done.1) | copy-start | bytes 13369348
  99.8 12.7 %copy-start.5 = (f32[512,2048]{1,0:T(8,128)S(1)}, f32[512,2048]{1,0:T(8,128)}, u32[]{:S(2)}) copy-start(f32[512,2048]{1,0:T(8,128)} %copy-done.3) | copy-start | bytes 12582916
Sparse Core Ops, SparseCore 0:
  99.7 31.1 reduce-scatter.1
Sparse Core Ops, SparseCore 1:
  139.7 174.5 all-reduce.5
where the time goes:
time: 327 us; the launch traced here: 326 us
  waiting for transfers between devices  179 us (55%)
  other arithmetic  81 us (25%)
  matrix products  17.1 us (5%)
  between operations  17.1 us (5%)
  starting transfers between devices  12.4 us (4%)
  local copies, waits for them, and re-layouts  11.7 us (4%)
  blocking collectives  8.1 us (2%)
    psum x1, waiting for transfers between devices, per_device(): lax.psum((query_part, kernel_part), ('tm', 'rec'))  172 us
    reduce_sum x5, other arithmetic, per_device(): jnp.sum(map_grad * padded[offset:offset + row_count], axis=0)  28.7 us
    reduce_max x1, other arithmetic, row_softmax(): local_top = jnp.max(smooth, axis=1)  22.3 us
    convert_element_type x1, other arithmetic, per_device(): jnp.where(is_valid[:, None], score_grad, 0.0).astype(jnp.bfloat16)  18.4 us
    ppermute x2, starting transfers between devices, with_halo(): before = lax.ppermute(last, axis, up)  9.51 us
    unnamed x1, blocking collectives  8.1 us
    dot_general x1, matrix products, per_device(): lax.dot_general(score_grad, frame_rows, (((0,), (0,)), ((), ())), preferr...  7.19 us
    unnamed x28, local copies, waits for them, and re-layouts  7.14 us
  transfers between devices with their start and end apart: 6, of which 3 were waited for; matrix products, arithmetic and copies ran while one was open for 14% of the time, Pallas kernels for 0%

commit v1 on v0

--- a/solution.py
+++ b/solution.py
@@ -98,7 +98,12 @@
             for offset in range(tap_count)
         ]
     )
-    query_whole, grad_kernel = lax.psum((query_part, kernel_part), ("tm", "rec"))
+
+    def carry_the_cubes(field_in):
+        mixed_arr = lax.psum(lax.psum(field_in, "rec"), axis_name="tm")
+        return mixed_arr
+
+    query_whole, grad_kernel = carry_the_cubes((query_part, kernel_part))
     col_count = width // lax.axis_size("rec")
     query_cols = lax.dynamic_slice_in_dim(
         query_whole, lax.axis_index("rec") * col_count, col_count, 1

time: 327 us -> 596 us (1.82)
  waiting for transfers between devices: 179 us -> 458 us
  other arithmetic: 81 us -> 71 us
    psum x1 -> x2, waiting for transfers between devices: 172 us -> 452 us  [carry_the_cubes(): mixed_arr = lax.psum(lax.psum(field_in, 'rec'), axis_name='tm')]
    reduce_sum x5, other arithmetic: 28.7 us -> 19.4 us  [per_device(): jnp.sum(map_grad * padded[offset:offset + row_count], axis=0)]
  transfers between devices with their start and end apart: 6 -> 7, of which waited for: 3 -> 4; matrix products, arithmetic and copies ran while one was open for 14% -> 2% of each run, Pallas kernels for 0% -> 0%
where the time goes in v1:
time: 596 us
  waiting for transfers between devices  458 us (77%)
  other arithmetic  71 us (12%)
  between operations  17.1 us (3%)
  matrix products  16.1 us (3%)
  local copies, waits for them, and re-layouts  13 us (2%)
  starting transfers between devices  12.2 us (2%)
  blocking collectives  8.09 us (1%)
    psum x2, waiting for transfers between devices, carry_the_cubes(): mixed_arr = lax.psum(lax.psum(field_in, 'rec'), axis_name='tm')  452 us
    reduce_max x1, other arithmetic, row_softmax(): local_top = jnp.max(smooth, axis=1)  22.3 us
    reduce_sum x5, other arithmetic, per_device(): jnp.sum(map_grad * padded[offset:offset + row_count], axis=0)  19.4 us
    convert_element_type x1, other arithmetic, per_device(): jnp.where(is_valid[:, None], score_grad, 0.0).astype(jnp.bfloat16)  17.6 us
  transfers between devices with their start and end apart: 7, of which 4 were waited for; matrix products, arithmetic and copies ran while one was open for 2% of the time, Pallas kernels for 0%

profile of v1, /device:TPU:0, one launch (start us, length us, event | category | flops | bytes accessed | tf_op | source)
XLA Modules:
  0.0 595.9 jit_solution(15466997710117592334)
XLA Ops:
  8.0 0.0 copy-start
  8.0 0.0 all-reduce.8.cloned.1.call-start
  8.1 0.8 slice_bitcast_fusion.1
  8.9 4.9 collective-permute-start.2
  13.8 1.3 collective-permute-start.3
  15.8 0.0 copy-done
  15.8 0.0 copy-start.7
  15.8 0.0 copy-start.9
  15.8 0.0 copy-start.8
  15.8 4.6 multiply_select_fusion
  20.5 0.0 copy-start.1
  20.5 1.9 copy-done.1
  22.4 4.6 collective-permute-start
  27.0 1.3 collective-permute-start.1
  28.3 0.0 copy-done.7
  28.3 0.1 fusion.176
  28.4 0.1 fusion.175
  28.5 0.0 copy-done.9
  28.6 0.6 dynamic-slice
  29.8 0.0 collective-permute-done.2
  29.8 0.0 collective-permute-done.3
  29.8 0.0 copy-done.8
  29.8 0.1 pad_add_fusion
  29.9 0.0 copy-start.2
  29.9 2.1 collective-permute-done
  32.0 4.1 collective-permute-done.1
  36.1 2.8 pad_maximum_fusion.2
  38.9 0.0 copy-done.2
  38.9 22.3 %fusion.172 = (f32[544]{0:T(1024)S(1)}, f32[544,2048]{1,0:T(8,128)S(1)}) fusion(f32[32,2048]{1,0:T(8,128)S(1)} %collective-permute-done.1, f32[512,2048]{1,0:T(8,128)S(1)} %copy-done.2, f32[2048]{0:T(1024)S(1)} %bitcast.110, f32[576,2048]{1,0:T(8,128)S(1)} %pad_maximum_fusion.2, f32[2048]{0:T(1024)S(1)} %bitcast.112, f32[2048]{0:T(1024)S(1)} %bitcast.116, ...), kind=kLoop, calls=%fused_computation.285 | loop fusion | flops 75759072 | bytes 147597440 | tf_op jit(solution)/shard_map/reduce_max | solution.py:49
  61.1 0.0 copy-start.4
  61.2 2.0 copy-done.4
  63.2 0.7 exponential_reduce_fusion
  63.9 0.3 dynamic-update-slice
  64.2 0.3 dynamic-update-slice.1
  64.5 8.1 %all-reduce.4 = (f32[1088]{0:T(1024)S(1)}, f32[1088]{0:T(1024)S(1)}) all-reduce(f32[1088]{0:T(1024)S(1)} %dynamic-update-slice.1, f32[1088]{0:T(1024)S(1)} %dynamic-update-slice), channel_id=3, replica_groups=mesh['tm'=4,'query'=2,'rec'=4] {'query'}, use_global_device_ids=true, to_apply=%add.1 | all-reduce | flops 2176 | bytes 17408
  72.6 0.1 fusion.168
  72.7 3.1 subtract_select_fusion
  75.8 17.6 %fusion.132 = bf16[512,2048]{1,0:T(8,128)(2,1)S(1)} fusion(f32[544,2048]{1,0:T(8,128)S(1)} %subtract_select_fusion, f32[2048]{0:T(1024)S(1)} %bitcast.111, f32[2048]{0:T(1024)S(1)} %bitcast.113, f32[2048]{0:T(1024)S(1)} %bitcast.117, f32[2048]{0:T(1024)S(1)} %bitcast.119, f32[2048]{0:T(1024)S(1)} %bitcast.121, f32[2048]{0:T(1024)S(1)} %bitcast.123, ...), kind=kLoop, calls=%fused_computation.201 | loop fusion | flops 70254592 | bytes 140780032 | tf_op jit(solution)/shard_map/convert_element_type | solution.py:88
  93.4 0.0 copy-start.5
  93.5 0.0 copy-start.3
  93.5 5.6 fusion.164
  99.1 0.0 copy-done.5
  99.1 0.0 copy-done.3
  99.1 3.2 fusion.129
  102.3 3.8 fusion.78
  106.1 3.8 fusion.81
  110.0 5.4 fusion.75
  115.4 3.2 fusion.126
  118.6 3.5 stack.135
  122.1 0.0 copy-start.6
  122.1 0.0 all-reduce.8.cloned.1.call-update
  122.2 0.0 reduce-scatter.2.cloned.1.call-start
  122.2 1.5 copy-done.6
  123.7 5.9 fusion.177
  129.6 0.0 reduce-scatter.2.cloned.1.call-update
  129.6 0.0 all-reduce.10.cloned.1.call-start
  129.7 150.1 %all-reduce.8.cloned.1.call-done = (f32[2048,1024]{1,0:T(8,128)}, f32[33,2048]{1,0:T(8,128)}) async-done(((f32[2048,1024]{1,0:T(8,128)}, f32[33,2048]{1,0:T(8,128)}), (f32[2048,1024]{1,0:T(8,128)}, f32[33,2048]{1,0:T(8,128)})) %all-reduce.8.cloned.1.call-update) | async-done | bytes 8658960 | tf_op jit(solution)/shard_map/psum | solution.py:103
  279.7 0.0 all-reduce.10.cloned.1.call-update
  279.8 0.0 reduce-scatter.2.cloned.1.call-done
  279.8 2.1 fusion.167
  281.9 302.0 %all-reduce.10.cloned.1.call-done = (f32[2048,1024]{1,0:T(8,128)}, f32[33,2048]{1,0:T(8,128)}) async-done(((f32[2048,1024]{1,0:T(8,128)}, f32[33,2048]{1,0:T(8,128)}), (f32[2048,1024]{1,0:T(8,128)}, f32[33,2048]{1,0:T(8,128)})) %all-reduce.10.cloned.1.call-update) | async-done | bytes 8658960 | tf_op jit(solution)/shard_map/psum | solution.py:103
  584.0 2.7 multiply_convert_fusion
  586.7 1.7 copy.15
  (6 shorter events, 0.1 us)
Async XLA Ops:
  8.0 7.8 %copy-start = (bf16[1,512,1024]{2,1,0:T(8,128)(2,1)S(1)}, bf16[1,512,1024]{2,1,0:T(8,128)(2,1)}, u32[]{:S(2)}) copy-start(bf16[1,512,1024]{2,1,0:T(8,128)(2,1)} %param.5) | copy-start | bytes 3145732
  8.0 271.7 %all-reduce.8.cloned.1.call-start = ((), (), s32[]{:S(2)}) async-start(), calls=%async_computation.2 | async-start | bytes 17432576 | tf_op jit(solution)/shard_map/psum | solution.py:103
  8.9 20.9 %collective-permute-start.2 = (s32[16]{0:T(128)S(1)}, s32[16]{0:T(128)S(1)}, u32[]{:S(2)}, u32[]{:S(2)}) collective-permute-start(s32[16]{0:T(128)S(1)} %get-tuple-element.103), channel_id=1, source_target_pairs={{0,8},{8,16},{16,24},{1,9},{9,17},{17,25},{2,10},{10,18},{18,26},{... | collective-permute-start | bytes 200 | tf_op jit(solution)/shard_map/ppermute | solution.py:25
  13.8 16.0 %collective-permute-start.3 = (s32[16]{0:T(128)S(1)}, s32[16]{0:T(128)S(1)}, u32[]{:S(2)}, u32[]{:S(2)}) collective-permute-start(s32[16]{0:T(128)S(1)} %get-tuple-element.104), channel_id=1, source_target_pairs={{8,0},{16,8},{24,16},{9,1},{17,9},{25,17},{10,2},{18,10},{26,18},{... | collective-permute-start | bytes 200 | tf_op jit(solution)/shard_map/ppermute | solution.py:26
  15.8 12.5 %copy-start.7 = (f32[33,2048]{1,0:T(8,128)S(1)}, f32[33,2048]{1,0:T(8,128)}, u32[]{:S(2)}) copy-start(f32[33,2048]{1,0:T(8,128)} %param.7) | copy-start | bytes 811012
  15.8 12.7 %copy-start.9 = (u32[32]{0:T(128)S(1)}, u32[32]{0:T(128)}, u32[]{:S(2)}) copy-start(u32[32]{0:T(128)} %constant.48) | copy-start | bytes 388
  15.8 14.0 %copy-start.8 = (s32[1,512]{1,0:T(1,128)S(1)}, s32[1,512]{1,0:T(1,128)}, u32[]{:S(2)}) copy-start(s32[1,512]{1,0:T(1,128)} %param.8) | copy-start | bytes 6148
  20.5 1.9 copy-start.1
  22.4 9.5 %collective-permute-start = (f32[32,2048]{1,0:T(8,128)S(1)}, f32[32,2048]{1,0:T(8,128)S(1)}, u32[]{:S(2)}, u32[]{:S(2)}) collective-permute-start(f32[32,2048]{1,0:T(8,128)S(1)} %get-tuple-element.68), channel_id=1, source_target_pairs={{0,8},{8,16},{16,24},{1,9},{9,17},{17,25},{2,10},{10,18},{18,26},{... | collective-permute-start | bytes 786440 | tf_op jit(solution)/shard_map/ppermute | solution.py:25
  27.0 9.1 %collective-permute-start.1 = (f32[32,2048]{1,0:T(8,128)S(1)}, f32[32,2048]{1,0:T(8,128)S(1)}, u32[]{:S(2)}, u32[]{:S(2)}) collective-permute-start(f32[32,2048]{1,0:T(8,128)S(1)} %get-tuple-element.69), channel_id=1, source_target_pairs={{8,0},{16,8},{24,16},{9,1},{17,9},{25,17},{10,2},{18,10},{26,18},{... | collective-permute-start | bytes 786440 | tf_op jit(solution)/shard_map/ppermute | solution.py:26
  29.9 9.0 %copy-start.2 = (f32[512,2048]{1,0:T(8,128)S(1)}, f32[512,2048]{1,0:T(8,128)}, u32[]{:S(2)}) copy-start(f32[512,2048]{1,0:T(8,128)} %copy-done.1) | copy-start | bytes 12582916
  61.1 2.0 copy-start.4
  93.4 5.7 copy-start.5
  93.5 5.7 copy-start.3
  122.1 1.6 copy-start.6
  122.2 157.6 %reduce-scatter.2.cloned.1.call-start = ((), (), s32[]{:S(2)}) async-start(), calls=%async_computation.1 | async-start | bytes 3145728 | tf_op jit(solution)/shard_map/reduce_scatter | solution.py:90
  129.6 454.3 %all-reduce.10.cloned.1.call-start = ((), (), s32[]{:S(2)}) async-start(), calls=%async_computation.3 | async-start | bytes 17432576 | tf_op jit(solution)/shard_map/psum | solution.py:103
Sparse Core Ops, SparseCore 0:
  122.3 157.4 all-reduce.7
  282.4 301.5 all-reduce.9
Sparse Core Ops, SparseCore 1:
  129.7 31.1 reduce-scatter.1
